TPU v7x, 128 devices: a whole 4x4x4 slice. The times are simulated.
128 devices in a mesh: row: 16 (over y, x), col: 4 (over z), dp: 2 (over core).
Axes of the slice: x: 4, y: 4, z: 4, core: 2. Of those that a mesh axis runs over, the one named last changes fastest.
Arguments:
- inputs: bfloat16 [1024, 8192], P(('col', 'dp'), 'row'), may hold values from -6 to 6
- gate_weight: bfloat16 [8192, 14336], P('row', 'col'), may hold values from -0.0625 to 0.0625
- up_weight: bfloat16 [8192, 14336], P('row', 'col'), may hold values from -0.0625 to 0.0625
- down_weight: bfloat16 [14336, 8192], P('col', 'row'), may hold values from -0.046875 to 0.046875
- reward_head: bfloat16 [8192], P('row'), may hold values from -0.0625 to 0.0625
- upstream: bfloat16 [1024, 8192], P(('col', 'dp'), 'row'), may hold values from -0.59765625 to 0.59765625
- labels: int32 [1024], P(('col', 'dp')), may hold values from 0 to 1
- label_mask: int32 [1024], P(('col', 'dp')), may hold values 0 or 1
Outputs:
- gate_grad: float32 [8192, 14336], P(('row', 'dp'), 'col')
- up_grad: float32 [8192, 14336], P(('row', 'dp'), 'col')
- down_grad: float32 [14336, 8192], P(('col', 'dp'), 'row')
- input_grad: float32 [1024, 8192], P(('col', 'dp'), 'row')
All inputs are finite; a program needn't handle non-finite values. No bound on the sum of `label_mask` on one device may be relied on, other than what follows from the above.
Results may differ from a plain program's by a relative error of at most 0.035.
Values may be sent and summed in bfloat16 or wider, within the bound.
No kernel may reach another device: no remote copies, remote signals or barrier semaphores. Data moves between devices by JAX's collectives and lax.ppermute only.
A program may use at most 128 MiB of HBM per device.

v0:
```python
import jax
import jax.numpy as jnp
from jax import lax
from jax.sharding import PartitionSpec as P

reward_weight = 8.0
BF = jnp.bfloat16
F32 = jnp.float32


def transpose_product(left, right):
    return lax.dot_general(left, right, (((0,), (0,)), ((), ())), preferred_element_type=F32)


def right_transpose(left, right):
    return lax.dot_general(left, right, (((1,), (1,)), ((), ())), preferred_element_type=F32)


def per_device(
    inputs, gate_weight, up_weight, down_weight, reward_head, upstream, labels, label_mask
):
    tokens, depth = inputs.shape
    half = gate_weight.shape[1] // 2
    n_row = lax.axis_size("row")
    core = lax.axis_index("dp")
    row = lax.axis_index("row")
    token_axes = ("col", "dp")
    tags = jnp.stack([labels, label_mask], axis=1).astype(BF)
    tags = jnp.pad(tags, ((0, 0), (0, 126)))
    packed = jnp.concatenate([inputs, upstream, tags], axis=1)
    everyone = lax.all_gather(packed, token_axes, axis=0, tiled=True)
    x_all = everyone[:, :depth]
    upstream_all = everyone[:, depth : 2 * depth]
    total = x_all.shape[0]
    mine = total // n_row
    gate_half = lax.dynamic_slice_in_dim(gate_weight, core * half, half, 1)
    up_half = lax.dynamic_slice_in_dim(up_weight, core * half, half, 1)
    down_half = lax.dynamic_slice_in_dim(down_weight, core * half, half, 0)
    head_value = reward_head.astype(F32)
    head_hidden = jnp.dot(down_half.astype(F32), head_value, precision=lax.Precision.HIGHEST)
    head_inputs = jnp.dot(x_all.astype(F32), head_value, precision=lax.Precision.HIGHEST)
    per_token = half // mine
    extras = jnp.concatenate(
        [
            head_inputs[:, None],
            jnp.tile(head_hidden.reshape(mine, per_token), (n_row, 1)),
            jnp.zeros((total, 127 - per_token), F32),
        ],
        axis=1,
    )
    partial = jnp.concatenate(
        [
            jnp.dot(x_all, gate_half, preferred_element_type=F32).astype(BF),
            jnp.dot(x_all, up_half, preferred_element_type=F32).astype(BF),
            right_transpose(upstream_all, down_half).astype(BF),
            extras.astype(BF),
        ],
        axis=1,
    )
    summed = lax.psum_scatter(partial, "row", scatter_dimension=0, tiled=True).astype(F32)
    gate = summed[:, :half]
    upper = summed[:, half : 2 * half]
    grad_upstream = summed[:, 2 * half : 3 * half]
    extra = summed[:, 3 * half :]
    head_hidden = extra[:, 1 : 1 + per_token].reshape(half)
    sigmoid_gate = jax.nn.sigmoid(gate)
    hidden = (gate * sigmoid_gate * upper).astype(BF)
    score = extra[:, 0] + lax.psum(
        jnp.sum(hidden.astype(F32) * head_hidden[None, :], axis=1), token_axes
    )
    own_tags = lax.dynamic_slice_in_dim(everyone[:, 2 * depth :], row * mine, mine, 0).astype(F32)
    slope = reward_weight * own_tags[:, 1] * (jax.nn.sigmoid(score) - own_tags[:, 0])
    grad_hidden = grad_upstream + slope[:, None] * head_hidden[None, :]
    grad_gate = (grad_hidden * upper * sigmoid_gate * (1.0 + gate * (1.0 - sigmoid_gate))).astype(
        BF
    )
    grad_upper = (grad_hidden * gate * sigmoid_gate).astype(BF)
    slope_high = slope.astype(BF)
    slope_low = (slope - slope_high.astype(F32)).astype(BF)
    slopes = jnp.pad(jnp.stack([slope_high, slope_low], axis=1), ((0, 0), (0, 126)))
    gathered = lax.all_gather(
        jnp.concatenate([hidden, grad_gate, grad_upper, slopes], axis=1), "row", axis=0, tiled=True
    )
    hidden_all = gathered[:, :half]
    grad_gate_all = gathered[:, half : 2 * half]
    grad_upper_all = gathered[:, 2 * half : 3 * half]
    slope_all = gathered[:, 3 * half].astype(F32) + gathered[:, 3 * half + 1].astype(F32)
    input_part = right_transpose(grad_gate_all, gate_half) + right_transpose(
        grad_upper_all, up_half
    )
    input_sum = lax.psum_scatter(
        input_part.astype(BF), token_axes, scatter_dimension=0, tiled=True
    ).astype(F32)
    place = (lax.axis_index("col") * 2 + core) * tokens
    own_slope = lax.dynamic_slice_in_dim(slope_all, place, tokens, 0)
    input_grad = upstream.astype(F32) + own_slope[:, None] * head_value[None, :] + input_sum
    grad_mixed = (upstream_all.astype(F32) + slope_all[:, None] * head_value[None, :]).astype(BF)
    down_grad = transpose_product(hidden_all, grad_mixed)

    def both_halves(part):
        keep = lax.dynamic_slice_in_dim(part, core * (depth // 2), depth // 2, 0)
        send = lax.dynamic_slice_in_dim(part, (1 - core) * (depth // 2), depth // 2, 0)
        other = lax.ppermute(send.astype(BF), "dp", [(0, 1), (1, 0)]).astype(F32)
        first = core == 0
        return jnp.concatenate(
            [jnp.where(first, keep, other), jnp.where(first, other, keep)], axis=1
        )

    gate_grad = both_halves(transpose_product(x_all, grad_gate_all))
    up_grad = both_halves(transpose_product(x_all, grad_upper_all))
    return (gate_grad, up_grad, down_grad, input_grad)


def solution(mesh):
    in_specs = (
        P(("col", "dp"), "row"),
        P("row", "col"),
        P("row", "col"),
        P("col", "row"),
        P("row"),
        P(("col", "dp"), "row"),
        P(("col", "dp")),
        P(("col", "dp")),
    )
    out_specs = (
        P(("row", "dp"), "col"),
        P(("row", "dp"), "col"),
        P(("col", "dp"), "row"),
        P(("col", "dp"), "row"),
    )
    return jax.shard_map(
        per_device, mesh=mesh, in_specs=in_specs, out_specs=out_specs, check_vma=False
    )
```

profile of v0, /device:TPU:0, one launch (start us, length us, event | category | flops | bytes accessed | tf_op | source)
XLA Modules:
  0.0 312.7 jit_solution(9628465307973189131)
XLA Ops:
  7.2 0.0 all-gather.3.cloned.1.call-start
  7.2 0.7 convert_bitcast_fusion.2
  7.9 0.1 copy.22
  8.0 1.7 fusion.37
  9.7 0.0 all-gather.3.cloned.1.call-update
  9.8 0.0 reduce-scatter.3.cloned.1.call-start
  9.8 0.7 reshape.23
  10.5 2.1 fusion.22
  12.6 0.1 reshape.22
  12.7 25.9 %all-gather.3.cloned.1.call-done = bf16[1024,1152]{1,0:T(8,128)(2,1)} async-done(((bf16[128,1152]{1,0:T(8,128)(2,1)}), bf16[1024,1152]{1,0:T(8,128)(2,1)}) %all-gather.3.cloned.1.call-update) | async-done | bytes 2359312 | tf_op jit(solution)/shard_map/all_gather | solution.py:31
  38.6 1.6 fusion.33
  40.2 0.2 broadcast_in_dim.14
  40.4 0.0 copy-start
  40.4 0.0 copy-start.4
  40.4 5.9 %convolution_convert_fusion = bf16[1024,1792]{1,0:T(8,128)(2,1)} fusion(bf16[3584,512]{1,0:T(8,128)(2,1)} %param.11, s32[]{:T(128)S(6)} %select_n.40, bf16[1024,1152]{1,0:T(8,128)(2,1)} %all-gather.3.cloned.1.call-done), kind=kOutput, calls=%fused_computation | convolution fusion | flops 1880883200 | bytes 6553604 | tf_op jit(solution)/shard_map/dot_general | solution.py:16
  46.3 0.0 copy-done
  46.4 0.0 copy-done.4
  46.4 3.9 %convolution_convert_fusion.1 = bf16[1024,1792]{1,0:T(8,128)(2,1)} fusion(bf16[512,3584]{1,0:T(8,128)(2,1)S(1)} %copy-done.4, s32[]{:T(128)S(6)} %select_n.40, bf16[1024,1152]{1,0:T(8,128)(2,1)S(1)} %copy-done), kind=kOutput, calls=%fused_computation.1 | convolution fusion | flops 1880883200 | bytes 6553604 | tf_op jit(solution)/shard_map/dot_general | solution.py:54
  50.3 0.0 copy-done.5
  50.3 3.9 %convolution_convert_fusion.2 = bf16[1024,1792]{1,0:T(8,128)(2,1)} fusion(bf16[512,3584]{1,0:T(8,128)(2,1)S(1)} %copy-done.5, s32[]{:T(128)S(6)} %select_n.40, bf16[1024,1152]{1,0:T(8,128)(2,1)S(1)} %copy-done), kind=kOutput, calls=%fused_computation.2 | convolution fusion | flops 1880883200 | bytes 6553604 | tf_op jit(solution)/shard_map/dot_general | solution.py:53
  54.3 18.4 %concatenate.19 = bf16[1024,5504]{1,0:T(8,128)(2,1)} concatenate(bf16[1024,1792]{1,0:T(8,128)(2,1)} %convolution_convert_fusion.2, bf16[1024,1792]{1,0:T(8,128)(2,1)} %convolution_convert_fusion.1, bf16[1024,1792]{1,0:T(8,128)(2,1)} %convolution_convert_fusion, bf16[1024,1]{1,0:T(8,128)(2,1)S(1)} %broadcast_in_dim.14, bf16[1024,28]{1,0:T(8,128)(2,1)S(1)} %bitcast.12, ...), dimensions={1} | concatenate | bytes 22544384 | tf_op jit(solution)/shard_map/concatenate | solution.py:51
  72.6 0.0 reduce-scatter.3.cloned.1.call-update
  72.7 0.0 all-gather.5.cloned.1.call-start
  72.7 0.9 slice-done
  73.6 0.2 slice_reduce_fusion
  73.8 90.5 %reduce-scatter.3.cloned.1.call-done = bf16[64,5504]{1,0:T(8,128)(2,1)} async-done(((bf16[1024,5504]{1,0:T(8,128)(2,1)}), bf16[64,5504]{1,0:T(8,128)(2,1)}) %reduce-scatter.3.cloned.1.call-update) | async-done | bytes 704528 | tf_op jit(solution)/shard_map/reduce_scatter | solution.py:60
  164.3 0.8 slice.71
  165.1 0.1 mul.114
  165.2 1.2 convert_element_type.87
  166.4 0.1 slice_reduce_fusion.1
  166.5 0.0 copy-start.3
  166.5 0.2 multiply_reduce_fusion
  166.8 14.2 %psum.7 = f32[64]{0:T(128)S(1)} all-reduce(f32[64]{0:T(128)S(1)} %get-tuple-element.8), channel_id=1, replica_groups=mesh['row'=16,'col'=4,'dp'=2] {'col','dp'}, use_global_device_ids=true, to_apply=%region_2.3 | all-reduce | flops 64 | bytes 512 | tf_op jit(solution)/shard_map/psum | solution.py:68
  181.0 0.3 multiply_convert_fusion.1
  181.3 0.1 copy.21
  181.4 0.9 fusion.29
  182.3 0.0 all-gather.5.cloned.1.call-update
  182.3 0.0 reduce-scatter.5.cloned.1.call-start
  182.4 0.0 copy-done.3
  182.4 80.0 %all-gather.5.cloned.1.call-done = bf16[1024,5504]{1,0:T(8,128)(2,1)} async-done(((bf16[64,5504]{1,0:T(8,128)(2,1)}), bf16[1024,5504]{1,0:T(8,128)(2,1)}) %all-gather.5.cloned.1.call-update) | async-done | bytes 11272208 | tf_op jit(solution)/shard_map/all_gather | solution.py:81
  262.4 4.8 %fusion.2 = f32[1024,512]{1,0:T(8,128)S(1)} fusion(bf16[1024,5504]{1,0:T(8,128)(2,1)} %all-gather.5.cloned.1.call-done, bf16[512,3584]{1,0:T(8,128)(2,1)} %param.10, s32[]{:T(128)S(6)} %select_n.40), kind=kOutput, calls=%fused_computation.7 | convolution fusion | flops 1879048192 | bytes 7602180 | tf_op jit(solution)/shard_map/dot_general | solution.py:16
  267.2 0.0 copy-done.6
  267.2 0.0 copy-start.1
  267.3 5.2 %add_convert_fusion = bf16[1024,512]{1,0:T(8,128)(2,1)} fusion(f32[1024,512]{1,0:T(8,128)S(1)} %fusion.2, bf16[512,3584]{1,0:T(8,128)(2,1)S(1)} %copy-done.6, s32[]{:T(128)S(6)} %select_n.40, bf16[1024,5504]{1,0:T(8,128)(2,1)} %all-gather.5.cloned.1.call-done), kind=kOutput, calls=%fused_computation.19 | convolution fusion | flops 1880096768 | bytes 8650756 | tf_op jit(solution)/shard_map/dot_general | solution.py:16
  272.5 0.0 reduce-scatter.5.cloned.1.call-update
  272.5 0.0 copy-done.1
  272.5 4.2 %fusion.4 = f32[512,1792]{1,0:T(8,128)S(1)} fusion(bf16[1024,5504]{1,0:T(8,128)(2,1)} %all-gather.5.cloned.1.call-done, bf16[1024,1152]{1,0:T(8,128)(2,1)S(1)} %copy-done.1), kind=kOutput, calls=%fused_computation.9 | convolution fusion | flops 1879048192 | bytes 8388608 | tf_op jit(solution)/shard_map/dot_general | solution.py:12
  276.7 0.1 dynamic-slice_convert_fusion
  276.8 0.3 collective-permute-start.1
  277.1 4.1 %fusion.8 = f32[512,1792]{1,0:T(8,128)S(1)} fusion(bf16[1024,5504]{1,0:T(8,128)(2,1)} %all-gather.5.cloned.1.call-done, bf16[1024,1152]{1,0:T(8,128)(2,1)S(1)} %copy-done.1), kind=kOutput, calls=%fused_computation.13 | convolution fusion | flops 1879048192 | bytes 8388608 | tf_op jit(solution)/shard_map/dot_general | solution.py:12
  281.2 0.1 dynamic-slice_convert_fusion.1
  281.3 0.6 collective-permute-start
  281.9 1.5 convert_add_fusion
  283.4 0.1 dynamic-slice_reduce_fusion
  283.6 6.1 %fusion = f32[1792,512]{1,0:T(8,128)} fusion(bf16[1024,5504]{1,0:T(8,128)(2,1)} %all-gather.5.cloned.1.call-done, f32[512]{0:T(512)S(1)} %convert_element_type.103, f32[1024]{0:T(1024)S(1)} %get-tuple-element.11, bf16[1024,1152]{1,0:T(8,128)(2,1)S(1)} %copy-done.1), kind=kOutput, calls=%fused_computation.3 | convolution fusion | flops 1881145344 | bytes 8394752 | tf_op jit(solution)/shard_map/dot_general | solution.py:12
  289.6 0.0 collective-permute-done.1
  289.6 0.3 convert_select_fusion.1
  289.9 2.3 pad_maximum_fusion.1
  292.2 0.0 collective-permute-done
  292.2 0.2 convert_select_fusion.3
  292.5 0.0 copy-start.2
  292.5 2.3 pad_maximum_fusion
  294.8 9.6 %reduce-scatter.5.cloned.1.call-done = bf16[128,512]{1,0:T(8,128)(2,1)} async-done(((bf16[1024,512]{1,0:T(8,128)(2,1)}), bf16[128,512]{1,0:T(8,128)(2,1)}) %reduce-scatter.5.cloned.1.call-update) | async-done | bytes 131088 | tf_op jit(solution)/shard_map/reduce_scatter | solution.py:91
  304.4 1.7 convert_add_fusion.1
  (13 shorter events, 0.1 us)
Async XLA Ops:
  7.2 31.4 %all-gather.3.cloned.1.call-start = ((), (), s32[]{:S(2)}) async-start(), calls=%async_computation.2 | async-start | bytes 2654208 | tf_op jit(solution)/shard_map/all_gather | solution.py:31
  9.8 154.5 %reduce-scatter.3.cloned.1.call-start = ((), (), s32[]{:S(2)}) async-start(), calls=%async_computation.3 | async-start | bytes 11976704 | tf_op jit(solution)/shard_map/reduce_scatter | solution.py:60
  40.4 5.9 %copy-start = (bf16[1024,1152]{1,0:T(8,128)(2,1)S(1)}, bf16[1024,1152]{1,0:T(8,128)(2,1)}, u32[]{:S(2)}) copy-start(bf16[1024,1152]{1,0:T(8,128)(2,1)} %all-gather.3.cloned.1.call-done) | copy-start | bytes 7077892
  40.4 5.9 %copy-start.4 = (bf16[512,3584]{1,0:T(8,128)(2,1)S(1)}, bf16[512,3584]{1,0:T(8,128)(2,1)}, u32[]{:S(2)}) copy-start(bf16[512,3584]{1,0:T(8,128)(2,1)} %param.10) | copy-start | bytes 11010052
  46.4 3.9 %copy-start.5 = (bf16[512,3584]{1,0:T(8,128)(2,1)S(1)}, bf16[512,3584]{1,0:T(8,128)(2,1)}, u32[]{:S(2)}) copy-start(bf16[512,3584]{1,0:T(8,128)(2,1)} %param.9) | copy-start | bytes 11010052
  72.6 0.9 slice-start
  72.7 189.7 %all-gather.5.cloned.1.call-start = ((), (), s32[]{:S(2)}) async-start(), calls=%async_computation.4 | async-start | bytes 11976704 | tf_op jit(solution)/shard_map/all_gather | solution.py:81
  166.5 15.9 %copy-start.3 = (bf16[512]{0:T(512)(128)(2,1)S(1)}, bf16[512]{0:T(512)(128)(2,1)}, u32[]{:S(2)}) copy-start(bf16[512]{0:T(512)(128)(2,1)} %param.12) | copy-start | bytes 3076
  182.3 122.1 %reduce-scatter.5.cloned.1.call-start = ((), (), s32[]{:S(2)}) async-start(), calls=%async_computation.5 | async-start | bytes 1179648 | tf_op jit(solution)/shard_map/reduce_scatter | solution.py:91
  262.4 4.9 %copy-start.6 = (bf16[512,3584]{1,0:T(8,128)(2,1)S(1)}, bf16[512,3584]{1,0:T(8,128)(2,1)}, u32[]{:S(2)}) copy-start(bf16[512,3584]{1,0:T(8,128)(2,1)} %param.9) | copy-start | bytes 11010052
  267.2 5.3 %copy-start.1 = (bf16[1024,1152]{1,0:T(8,128)(2,1)S(1)}, bf16[1024,1152]{1,0:T(8,128)(2,1)}, u32[]{:S(2)}) copy-start(bf16[1024,1152]{1,0:T(8,128)(2,1)} %all-gather.3.cloned.1.call-done) | copy-start | bytes 7077892
  276.8 12.8 %collective-permute-start.1 = (bf16[256,1792]{1,0:T(8,128)(2,1)S(1)}, bf16[256,1792]{1,0:T(8,128)(2,1)S(1)}, u32[]{:S(2)}, u32[]{:S(2)}) collective-permute-start(bf16[256,1792]{1,0:T(8,128)(2,1)S(1)} %dynamic-slice_convert_fusion), channel_id=1, source_target_pairs={{0,1},{1,0},{2,3},{3,2},{4,5},{5,4},{6,7},{7,6},{8,9},{9,8},{10,11... | collective-permute-start | bytes 2752520 | tf_op jit(solution)/shard_map/ppermute | solution.py:103
  281.3 10.9 %collective-permute-start = (bf16[256,1792]{1,0:T(8,128)(2,1)S(1)}, bf16[256,1792]{1,0:T(8,128)(2,1)S(1)}, u32[]{:S(2)}, u32[]{:S(2)}) collective-permute-start(bf16[256,1792]{1,0:T(8,128)(2,1)S(1)} %dynamic-slice_convert_fusion.1), channel_id=1, source_target_pairs={{0,1},{1,0},{2,3},{3,2},{4,5},{5,4},{6,7},{7,6},{8,9},{9,8},{10,11... | collective-permute-start | bytes 2752520 | tf_op jit(solution)/shard_map/ppermute | solution.py:103
  292.5 12.0 %copy-start.2 = (bf16[128,512]{1,0:T(8,128)(2,1)S(1)}, bf16[128,512]{1,0:T(8,128)(2,1)}, u32[]{:S(2)}) copy-start(bf16[128,512]{1,0:T(8,128)(2,1)} %param.13) | copy-start | bytes 393220
Sparse Core Ops, SparseCore 0:
  10.3 28.2 all-gather.2
  72.8 91.4 reduce-scatter.2
  182.4 79.9 all-gather.4
  272.6 31.7 reduce-scatter.4
where the time goes:
time: 314 us; the launch traced here: 313 us
  waiting for transfers between devices  206 us (66%)
  matrix products  41.9 us (13%)
  local copies, waits for them, and re-layouts  21.9 us (7%)
  blocking collectives  14.2 us (5%)
  between operations  14 us (4%)
  other arithmetic  13.6 us (4%)
    reduce_scatter x1, waiting for transfers between devices, per_device(): lax.psum_scatter(partial, 'row', scatter_dimension=0, tiled=True)  90.5 us
    all_gather x1, waiting for transfers between devices, per_device(): lax.all_gather(jnp.concatenate([hidden, grad_gate, grad_upper, slopes], a...  80 us
    all_gather x1, waiting for transfers between devices, per_device(): everyone = lax.all_gather(packed, token_axes, axis=0, tiled=True)  25.9 us
    concatenate x1, local copies, waits for them, and re-layouts, per_device(): jnp.concatenate([jnp.dot(x_all, gate_half, preferred_element_type=F32).as...  18.4 us
    dot_general x3, matrix products, right_transpose(): lax.dot_general(left, right, (((1,), (1,)), ((), ())), preferred_element_...  16 us
    dot_general x3, matrix products, transpose_product(): lax.dot_general(left, right, (((0,), (0,)), ((), ())), preferred_element_...  14.4 us
    psum x1, blocking collectives, per_device(): lax.psum(jnp.sum(hidden.astype(F32) * head_hidden[None, :], axis=1), toke...  14.2 us
    reduce_scatter x1, waiting for transfers between devices, per_device(): lax.psum_scatter(input_part.astype(BF), token_axes, scatter_dimension=0,...  9.63 us
  transfers between devices with their start and end apart: 6, of which 4 were waited for; matrix products, arithmetic and copies ran while one was open for 8% of the time, Pallas kernels for 0%

commit v1 on v0

--- a/solution.py
+++ b/solution.py
@@ -28,7 +28,9 @@
     tags = jnp.stack([labels, label_mask], axis=1).astype(BF)
     tags = jnp.pad(tags, ((0, 0), (0, 126)))
     packed = jnp.concatenate([inputs, upstream, tags], axis=1)
-    everyone = lax.all_gather(packed, token_axes, axis=0, tiled=True)
+    everyone = jnp.concatenate(
+        lax.all_to_all(jnp.stack([packed] * lax.axis_size(token_axes)), token_axes, 0, 0), axis=0
+    )
     x_all = everyone[:, :depth]
     upstream_all = everyone[:, depth : 2 * depth]
     total = x_all.shape[0]

time: 314 us -> 323 us (1.029)
  starting transfers between devices: 1 us -> 6.49 us
    all_to_all x0 -> x1, waiting for transfers between devices: none -> 27.7 us  [per_device(): lax.all_to_all(jnp.stack([packed] * lax.axis_size(token_axes)), token_axe...]
    all_gather x1 -> x0, waiting for transfers between devices: 25.9 us -> none  [per_device(): everyone = lax.all_gather(packed, token_axes, axis=0, tiled=True)]
    all_to_all x0 -> x1, starting transfers between devices: none -> 5.53 us  [per_device(): lax.all_to_all(jnp.stack([packed] * lax.axis_size(token_axes)), token_axe...]
  transfers between devices with their start and end apart: 6 -> 6, of which waited for: 4 -> 4; matrix products, arithmetic and copies ran while one was open for 8% -> 7% of each run, Pallas kernels for 0% -> 0%
where the time goes in v1:
time: 323 us; the launch traced here: 322 us
  waiting for transfers between devices  208 us (64%)
  matrix products  41.9 us (13%)
  local copies, waits for them, and re-layouts  24.9 us (8%)
  blocking collectives  14.2 us (4%)
  between operations  14 us (4%)
  other arithmetic  12.8 us (4%)
  starting transfers between devices  6.49 us (2%)
    reduce_scatter x1, waiting for transfers between devices, per_device(): lax.psum_scatter(partial, 'row', scatter_dimension=0, tiled=True)  90.5 us
    all_gather x1, waiting for transfers between devices, per_device(): lax.all_gather(jnp.concatenate([hidden, grad_gate, grad_upper, slopes], a...  80 us
    all_to_all x1, waiting for transfers between devices, per_device(): lax.all_to_all(jnp.stack([packed] * lax.axis_size(token_axes)), token_axe...  27.7 us
    concatenate x1, local copies, waits for them, and re-layouts, per_device(): jnp.concatenate([jnp.dot(x_all, gate_half, preferred_element_type=F32).as...  18.3 us
    dot_general x3, matrix products, right_transpose(): lax.dot_general(left, right, (((1,), (1,)), ((), ())), preferred_element_...  16 us
    dot_general x3, matrix products, transpose_product(): lax.dot_general(left, right, (((0,), (0,)), ((), ())), preferred_element_...  14.4 us
    psum x1, blocking collectives, per_device(): lax.psum(jnp.sum(hidden.astype(F32) * head_hidden[None, :], axis=1), toke...  14.2 us
    reduce_scatter x1, waiting for transfers between devices, per_device(): lax.psum_scatter(input_part.astype(BF), token_axes, scatter_dimension=0,...  9.73 us
  transfers between devices with their start and end apart: 6, of which 4 were waited for; matrix products, arithmetic and copies ran while one was open for 7% of the time, Pallas kernels for 0%

profile of v1, /device:TPU:0, one launch (start us, length us, event | category | flops | bytes accessed | tf_op | source)
XLA Modules:
  0.0 322.3 jit_solution(14505190267821144953)
XLA Ops:
  7.2 0.7 convert_bitcast_fusion.2
  7.9 0.1 copy.35
  8.0 1.0 fusion.37
  9.0 0.2 copy.31
  9.2 1.7 stack.35
  10.9 0.0 copy-start.3
  10.9 5.5 %all-to-all-start = ((bf16[8,128,1152]{1,2,0:T(8,128)(2,1)}), bf16[8,128,1152]{1,2,0:T(8,128)(2,1)S(1)}, u32[]{:S(2)}, u32[]{:S(2)}) async-start(bf16[8,128,1152]{1,2,0:T(8,128)(2,1)} %stack.35), calls=%async_computation | async-start | bytes 4718592 | tf_op jit(solution)/shard_map/all_to_all | solution.py:32
  16.4 0.0 reduce-scatter.3.cloned.1.call-start
  16.5 0.0 copy-done.3
  16.5 2.1 fusion.22
  18.6 0.1 reshape.28
  18.7 27.7 %all-to-all-done = bf16[8,128,1152]{1,2,0:T(8,128)(2,1)S(1)} async-done(((bf16[8,128,1152]{1,2,0:T(8,128)(2,1)}), bf16[8,128,1152]{1,2,0:T(8,128)(2,1)S(1)}, u32[]{:S(2)}, u32[]{:S(2)}) %all-to-all-start) | async-done | bytes 2359328 | tf_op jit(solution)/shard_map/all_to_all | solution.py:32
  46.5 2.6 copy.32
  49.0 1.6 fusion.33
  50.6 5.9 %convolution_convert_fusion = bf16[1024,1792]{1,0:T(8,128)(2,1)} fusion(bf16[3584,512]{1,0:T(8,128)(2,1)} %param.11, s32[]{:T(128)S(6)} %select_n.40, bf16[1024,1152]{1,0:T(8,128)(2,1)} %bitcast.14), kind=kOutput, calls=%fused_computation | convolution fusion | flops 1880883200 | bytes 6553604 | tf_op jit(solution)/shard_map/dot_general | solution.py:16
  56.6 0.2 broadcast_in_dim.14
  56.8 0.0 copy-done
  56.8 0.0 copy-done.4
  56.8 0.0 copy-start.5
  56.8 3.9 %convolution_convert_fusion.1 = bf16[1024,1792]{1,0:T(8,128)(2,1)} fusion(bf16[512,3584]{1,0:T(8,128)(2,1)S(1)} %copy-done.4, s32[]{:T(128)S(6)} %select_n.40, bf16[1024,1152]{1,0:T(8,128)(2,1)S(1)} %bitcast.15), kind=kOutput, calls=%fused_computation.1 | convolution fusion | flops 1880883200 | bytes 6553604 | tf_op jit(solution)/shard_map/dot_general | solution.py:56
  60.7 0.0 copy-done.5
  60.7 3.9 %convolution_convert_fusion.2 = bf16[1024,1792]{1,0:T(8,128)(2,1)} fusion(bf16[512,3584]{1,0:T(8,128)(2,1)S(1)} %copy-done.5, s32[]{:T(128)S(6)} %select_n.40, bf16[1024,1152]{1,0:T(8,128)(2,1)S(1)} %bitcast.16), kind=kOutput, calls=%fused_computation.2 | convolution fusion | flops 1880883200 | bytes 6553604 | tf_op jit(solution)/shard_map/dot_general | solution.py:55
  64.7 18.3 %concatenate.19 = bf16[1024,5504]{1,0:T(8,128)(2,1)} concatenate(bf16[1024,1792]{1,0:T(8,128)(2,1)} %convolution_convert_fusion.2, bf16[1024,1792]{1,0:T(8,128)(2,1)} %convolution_convert_fusion.1, bf16[1024,1792]{1,0:T(8,128)(2,1)} %convolution_convert_fusion, bf16[1024,1]{1,0:T(8,128)(2,1)S(1)} %broadcast_in_dim.14, bf16[1024,28]{1,0:T(8,128)(2,1)S(1)} %bitcast.21, ...), dimensions={1} | concatenate | bytes 22544384 | tf_op jit(solution)/shard_map/concatenate | solution.py:53
  83.1 0.0 reduce-scatter.3.cloned.1.call-update
  83.1 0.0 all-gather.2.cloned.1.call-start
  83.2 0.2 slice_reduce_fusion
  83.4 90.5 %reduce-scatter.3.cloned.1.call-done = bf16[64,5504]{1,0:T(8,128)(2,1)} async-done(((bf16[1024,5504]{1,0:T(8,128)(2,1)}), bf16[64,5504]{1,0:T(8,128)(2,1)}) %reduce-scatter.3.cloned.1.call-update) | async-done | bytes 704528 | tf_op jit(solution)/shard_map/reduce_scatter | solution.py:62
  173.9 0.8 slice.71
  174.7 0.1 mul.114
  174.8 1.2 convert_element_type.87
  176.0 0.1 slice_reduce_fusion.1
  176.1 0.3 multiply_reduce_fusion
  176.3 14.2 %psum.7 = f32[64]{0:T(128)S(1)} all-reduce(f32[64]{0:T(128)S(1)} %get-tuple-element.8), channel_id=1, replica_groups=mesh['row'=16,'col'=4,'dp'=2] {'col','dp'}, use_global_device_ids=true, to_apply=%region_2.3 | all-reduce | flops 64 | bytes 512 | tf_op jit(solution)/shard_map/psum | solution.py:70
  190.6 0.3 multiply_convert_fusion.1
  190.9 0.1 copy.34
  191.0 0.9 fusion.29
  191.9 0.0 all-gather.2.cloned.1.call-update
  191.9 0.0 reduce-scatter.5.cloned.1.call-start
  192.0 80.0 %all-gather.2.cloned.1.call-done = bf16[1024,5504]{1,0:T(8,128)(2,1)} async-done(((bf16[64,5504]{1,0:T(8,128)(2,1)}), bf16[1024,5504]{1,0:T(8,128)(2,1)}) %all-gather.2.cloned.1.call-update) | async-done | bytes 11272208 | tf_op jit(solution)/shard_map/all_gather | solution.py:83
  272.0 4.8 %fusion.2 = f32[1024,512]{1,0:T(8,128)S(1)} fusion(bf16[1024,5504]{1,0:T(8,128)(2,1)} %all-gather.2.cloned.1.call-done, bf16[512,3584]{1,0:T(8,128)(2,1)} %param.10, s32[]{:T(128)S(6)} %select_n.40), kind=kOutput, calls=%fused_computation.7 | convolution fusion | flops 1879048192 | bytes 7602180 | tf_op jit(solution)/shard_map/dot_general | solution.py:16
  276.9 0.0 copy-done.6
  276.9 0.0 copy-start.1
  276.9 5.3 %add_convert_fusion = bf16[1024,512]{1,0:T(8,128)(2,1)} fusion(f32[1024,512]{1,0:T(8,128)S(1)} %fusion.2, bf16[512,3584]{1,0:T(8,128)(2,1)S(1)} %copy-done.6, s32[]{:T(128)S(6)} %select_n.40, bf16[1024,5504]{1,0:T(8,128)(2,1)} %all-gather.2.cloned.1.call-done), kind=kOutput, calls=%fused_computation.19 | convolution fusion | flops 1880096768 | bytes 8650756 | tf_op jit(solution)/shard_map/dot_general | solution.py:16
  282.1 0.0 reduce-scatter.5.cloned.1.call-update
  282.1 0.0 copy-done.1
  282.2 4.2 %fusion.4 = f32[512,1792]{1,0:T(8,128)S(1)} fusion(bf16[1024,5504]{1,0:T(8,128)(2,1)} %all-gather.2.cloned.1.call-done, bf16[1024,1152]{1,0:T(8,128)(2,1)S(1)} %bitcast.18), kind=kOutput, calls=%fused_computation.9 | convolution fusion | flops 1879048192 | bytes 8388608 | tf_op jit(solution)/shard_map/dot_general | solution.py:12
  286.3 0.1 dynamic-slice_convert_fusion
  286.4 0.3 collective-permute-start.1
  286.7 4.1 %fusion.8 = f32[512,1792]{1,0:T(8,128)S(1)} fusion(bf16[1024,5504]{1,0:T(8,128)(2,1)} %all-gather.2.cloned.1.call-done, bf16[1024,1152]{1,0:T(8,128)(2,1)S(1)} %bitcast.19), kind=kOutput, calls=%fused_computation.13 | convolution fusion | flops 1879048192 | bytes 8388608 | tf_op jit(solution)/shard_map/dot_general | solution.py:12
  290.9 0.1 dynamic-slice_convert_fusion.1
  291.0 0.6 collective-permute-start
  291.5 1.4 convert_add_fusion
  293.0 0.1 dynamic-slice_reduce_fusion
  293.1 6.1 %fusion = f32[1792,512]{1,0:T(8,128)} fusion(bf16[1024,5504]{1,0:T(8,128)(2,1)} %all-gather.2.cloned.1.call-done, f32[512]{0:T(512)S(1)} %convert_element_type.103, f32[1024]{0:T(1024)S(1)} %get-tuple-element.11, bf16[1024,1152]{1,0:T(8,128)(2,1)S(1)} %bitcast.20), kind=kOutput, calls=%fused_computation.3 | convolution fusion | flops 1881145344 | bytes 8394752 | tf_op jit(solution)/shard_map/dot_general | solution.py:12
  299.1 0.0 collective-permute-done.1
  299.1 0.3 convert_select_fusion.1
  299.4 2.3 pad_maximum_fusion.1
  301.7 0.0 collective-permute-done
  301.7 0.2 convert_select_fusion.3
  302.0 0.0 copy-start.2
  302.0 2.3 pad_maximum_fusion
  304.3 9.7 %reduce-scatter.5.cloned.1.call-done = bf16[128,512]{1,0:T(8,128)(2,1)} async-done(((bf16[1024,512]{1,0:T(8,128)(2,1)}), bf16[128,512]{1,0:T(8,128)(2,1)}) %reduce-scatter.5.cloned.1.call-update) | async-done | bytes 131088 | tf_op jit(solution)/shard_map/reduce_scatter | solution.py:93
  314.0 0.0 copy-done.2
  314.0 1.7 convert_add_fusion.1
  (14 shorter events, 0.2 us)
Async XLA Ops:
  10.9 5.6 %copy-start.3 = (bf16[512]{0:T(512)(128)(2,1)S(1)}, bf16[512]{0:T(512)(128)(2,1)}, u32[]{:S(2)}) copy-start(bf16[512]{0:T(512)(128)(2,1)} %param.12) | copy-start | bytes 3076
  10.9 35.5 %all-to-all-start = ((bf16[8,128,1152]{1,2,0:T(8,128)(2,1)}), bf16[8,128,1152]{1,2,0:T(8,128)(2,1)S(1)}, u32[]{:S(2)}, u32[]{:S(2)}) async-start(bf16[8,128,1152]{1,2,0:T(8,128)(2,1)} %stack.35), calls=%async_computation | async-start | bytes 4718592 | tf_op jit(solution)/shard_map/all_to_all | solution.py:32
  16.4 157.4 %reduce-scatter.3.cloned.1.call-start = ((), (), s32[]{:S(2)}) async-start(), calls=%async_computation.3 | async-start | bytes 11976704 | tf_op jit(solution)/shard_map/reduce_scatter | solution.py:62
  50.6 6.2 %copy-start = (bf16[8,128,1152]{2,1,0:T(8,128)(2,1)S(1)}, bf16[8,128,1152]{2,1,0:T(8,128)(2,1)}, u32[]{:S(2)}) copy-start(bf16[8,128,1152]{2,1,0:T(8,128)(2,1)} %copy.32) | copy-start | bytes 7077892
  50.6 6.2 %copy-start.4 = (bf16[512,3584]{1,0:T(8,128)(2,1)S(1)}, bf16[512,3584]{1,0:T(8,128)(2,1)}, u32[]{:S(2)}) copy-start(bf16[512,3584]{1,0:T(8,128)(2,1)} %param.10) | copy-start | bytes 11010052
  56.8 3.9 %copy-start.5 = (bf16[512,3584]{1,0:T(8,128)(2,1)S(1)}, bf16[512,3584]{1,0:T(8,128)(2,1)}, u32[]{:S(2)}) copy-start(bf16[512,3584]{1,0:T(8,128)(2,1)} %param.9) | copy-start | bytes 11010052
  83.1 188.9 %all-gather.2.cloned.1.call-start = ((), (), s32[]{:S(2)}) async-start(), calls=%async_computation.4 | async-start | bytes 11976704 | tf_op jit(solution)/shard_map/all_gather | solution.py:83
  191.9 122.2 %reduce-scatter.5.cloned.1.call-start = ((), (), s32[]{:S(2)}) async-start(), calls=%async_computation.5 | async-start | bytes 1179648 | tf_op jit(solution)/shard_map/reduce_scatter | solution.py:93
  272.0 4.9 %copy-start.6 = (bf16[512,3584]{1,0:T(8,128)(2,1)S(1)}, bf16[512,3584]{1,0:T(8,128)(2,1)}, u32[]{:S(2)}) copy-start(bf16[512,3584]{1,0:T(8,128)(2,1)} %param.9) | copy-start | bytes 11010052
  276.9 5.3 %copy-start.1 = (bf16[8,128,1152]{2,1,0:T(8,128)(2,1)S(1)}, bf16[8,128,1152]{2,1,0:T(8,128)(2,1)}, u32[]{:S(2)}) copy-start(bf16[8,128,1152]{2,1,0:T(8,128)(2,1)} %copy.32) | copy-start | bytes 7077892
  286.4 12.7 %collective-permute-start.1 = (bf16[256,1792]{1,0:T(8,128)(2,1)S(1)}, bf16[256,1792]{1,0:T(8,128)(2,1)S(1)}, u32[]{:S(2)}, u32[]{:S(2)}) collective-permute-start(bf16[256,1792]{1,0:T(8,128)(2,1)S(1)} %dynamic-slice_convert_fusion), channel_id=1, source_target_pairs={{0,1},{1,0},{2,3},{3,2},{4,5},{5,4},{6,7},{7,6},{8,9},{9,8},{10,11... | collective-permute-start | bytes 2752520 | tf_op jit(solution)/shard_map/ppermute | solution.py:105
  291.0 10.8 %collective-permute-start = (bf16[256,1792]{1,0:T(8,128)(2,1)S(1)}, bf16[256,1792]{1,0:T(8,128)(2,1)S(1)}, u32[]{:S(2)}, u32[]{:S(2)}) collective-permute-start(bf16[256,1792]{1,0:T(8,128)(2,1)S(1)} %dynamic-slice_convert_fusion.1), channel_id=1, source_target_pairs={{0,1},{1,0},{2,3},{3,2},{4,5},{5,4},{6,7},{7,6},{8,9},{9,8},{10,11... | collective-permute-start | bytes 2752520 | tf_op jit(solution)/shard_map/ppermute | solution.py:105
  302.0 12.1 %copy-start.2 = (bf16[128,512]{1,0:T(8,128)(2,1)S(1)}, bf16[128,512]{1,0:T(8,128)(2,1)}, u32[]{:S(2)}) copy-start(bf16[128,512]{1,0:T(8,128)(2,1)} %param.13) | copy-start | bytes 393220
Sparse Core Ops, SparseCore 0:
  83.2 90.6 reduce-scatter.2
  192.0 79.9 all-gather.1
  282.3 31.7 reduce-scatter.4
